TPU v7x, 32 devices: a whole 2x2x4 slice. The times are simulated.
32 devices in a mesh: group: 16 (over z, y, core), tp: 2 (over x).
Axes of the slice: x: 2, y: 2, z: 4, core: 2. Of those that a mesh axis runs over, the one named last changes fastest.
Arguments:
- tokens: bfloat16 [8192, 3200], P('group', 'tp'), may hold values from -6 to 6
- norm_gain: bfloat16 [3200], P('tp'), may hold values from 0.25 to 1.75
- w_qkv: bfloat16 [3200, 3, 2048], P('group', None, 'tp'), may hold values from -1 to 1, as said below
- qk_gain: float32 [2, 2048], P(None, 'tp'), may hold values from 0.5 to 8
- w_out: bfloat16 [2048, 3200], P('tp', 'group'), may hold values from -0.125 to 0.125
- layer_scale: float32 [3200], P('tp'), may hold values from 0.3 to 1.5
- request: int32 [8192], P('group'), may hold values from 0 to 8191, as said below
- owner: int32 [8192, 1], P('group'), may hold values from 0 to 15; in each aligned block of 512 rows (0 to 511, 512 to 1023, ...) at most 64 rows name the same one
Outputs:
- routed: bfloat16 [16, 16, 64, 3200], P('group', None, None, 'tp')
Inputs may be any that keep to these rules, and one draw needn't show every extreme that they name: Requests never cross a block of 1024 rows starting at a multiple of 1024, and blocks share none; in each such block exactly one request holds rows on both sides of its middle, at most 128 on each side, exactly 128 on each side in the first block; the first row's number is 0 and the last row's is 8191. Among one group's 512 rows at most 64 name the same owner; some owner is named by exactly 64 rows of some group. `w_qkv`: column scales of the projections vary across the columns.
All inputs are finite; a program needn't handle non-finite values.
Results may differ from a plain program's by a relative error of at most 0.0117.
The roundings to bfloat16 on the way count: a program that leaves them out, or rounds other values in their place, can miss the bound.
Values may be sent and summed in bfloat16 or wider, within the bound.
A program may use at most 128 MiB of HBM per device.

v0:
```python
import math
import jax
import jax.numpy as jnp
from jax import lax
from jax.sharding import PartitionSpec as P

HD = 128
SHARE = 128


def swapped(value, axis, apart):
    mask = 2**apart
    pairs = [(source, source ^ mask) for source in range(lax.axis_size(axis))]
    return lax.ppermute(value, axis, pairs)


def shards(tokens, norm_gain, w_qkv, qk_gain, w_out, layer_scale, request, owner):
    rows = tokens.shape[0]
    feat_local = tokens.shape[1]
    tp_count = lax.axis_size("tp")
    group_count = lax.axis_size("group")
    local_width = w_qkv.shape[2]
    head_count = local_width // HD
    whole, gain_all = (
        lax.all_gather(tokens, "tp", axis=1, tiled=True),
        lax.all_gather(norm_gain.reshape(1, feat_local), "tp", axis=1, tiled=True),
    )
    xwide = whole.astype(jnp.float32)
    stat = jnp.mean(xwide * xwide, axis=-1, keepdims=True)
    normed = (xwide * lax.rsqrt(stat + 1e-06) * gain_all.astype(jnp.float32)).astype(jnp.bfloat16)
    piece = lax.all_gather(w_qkv, "group", axis=0, tiled=True)
    qkv = jnp.dot(
        normed, piece.reshape(piece.shape[0], 3 * local_width), preferred_element_type=jnp.float32
    ).reshape(rows, 3, local_width)
    query = qkv[:, 0, :]
    key_rows = qkv[:, 1, :]
    value = qkv[:, 2, :].astype(jnp.bfloat16)
    qsum, ksum = lax.psum(
        (jnp.sum(query * query, axis=-1), jnp.sum(key_rows * key_rows, axis=-1)), "tp"
    )
    total_width = local_width * tp_count
    qnorm = (query * lax.rsqrt(qsum / total_width + 1e-06)[:, None] * qk_gain[0]).astype(
        jnp.bfloat16
    )
    knorm = (key_rows * lax.rsqrt(ksum / total_width + 1e-06)[:, None] * qk_gain[1]).astype(
        jnp.bfloat16
    )
    parity = lax.axis_index("group") % 2
    seam = jnp.where(parity == 0, rows - SHARE, 0).astype(jnp.int32)
    key_window = lax.dynamic_slice_in_dim(knorm, seam, SHARE, 0)
    value_window = lax.dynamic_slice_in_dim(value, seam, SHARE, 0)
    id_window = lax.dynamic_slice_in_dim(request, seam, SHARE, 0)
    paired, paired_ids = swapped((jnp.stack([key_window, value_window]), id_window), "group", 0)
    all_keys = jnp.concatenate([knorm, paired[0]], axis=0)
    all_values = jnp.concatenate([value, paired[1]], axis=0)
    all_ids = jnp.concatenate([request, paired_ids], axis=0)
    qheads = qnorm.reshape(rows, head_count, HD)
    kheads = all_keys.reshape(rows + SHARE, head_count, HD)
    vheads = all_values.reshape(rows + SHARE, head_count, HD)
    scores = jnp.einsum(
        "qhd,khd->hqk", qheads, kheads, preferred_element_type=jnp.float32
    ) / math.sqrt(HD)
    same = request[:, None] == all_ids[None, :]
    scores = jnp.where(same[None], scores, -jnp.inf)
    top = jnp.max(scores, axis=-1, keepdims=True)
    expo = jnp.exp(scores - top)
    probs = (expo / jnp.sum(expo, axis=-1, keepdims=True)).astype(jnp.bfloat16)
    attended = jnp.einsum("hqk,khd->qhd", probs, vheads, preferred_element_type=jnp.float32)
    attended = attended.astype(jnp.bfloat16).reshape(rows, local_width)
    partial_terms = jnp.dot(
        attended,
        lax.all_gather(w_out, "group", axis=1, tiled=True),
        preferred_element_type=jnp.float32,
    )
    mine = lax.psum_scatter(
        partial_terms.astype(jnp.bfloat16), "tp", scatter_dimension=1, tiled=True
    ).astype(jnp.float32)
    mixed = (tokens.astype(jnp.float32) + layer_scale * mine).astype(jnp.bfloat16)
    capacity = max(2, 2 * rows // group_count)
    target = owner[:, 0]
    onehot = (target[:, None] == jnp.arange(group_count, dtype=jnp.int32)[None, :]).astype(
        jnp.int32
    )
    slot = jnp.sum((jnp.cumsum(onehot, axis=0) - onehot) * onehot, axis=-1)
    outbox = (
        jnp.zeros((group_count, capacity, feat_local), jnp.bfloat16).at[target, slot].set(mixed)
    )
    inbox = lax.all_to_all(outbox, "group", split_axis=0, concat_axis=0, tiled=True)
    return inbox[None]


def solution(mesh):
    in_specs = (
        P("group", "tp"),
        P("tp"),
        P("group", None, "tp"),
        P(None, "tp"),
        P("tp", "group"),
        P("tp"),
        P("group"),
        P("group", None),
    )
    out_specs = P("group", None, None, "tp")
    return jax.shard_map(shards, mesh=mesh, in_specs=in_specs, out_specs=out_specs, check_vma=False)
```

profile of v0, /device:TPU:1, one launch (start us, length us, event | category | flops | bytes accessed | tf_op | source)
XLA Modules:
  0.0 463.0 jit_solution(18097618292027908334)
XLA Ops:
  6.6 0.7 all-gather.5.cloned.1.call-update
  7.3 0.0 all-gather.7.cloned.1.call-start
  7.3 0.7 all-gather.7.cloned.1.call-update
  8.1 0.7 all-gather.9.cloned.1.call-update
  8.8 0.0 reduce-scatter.2.cloned.1.call-start
  8.8 0.1 dynamic_slice.11
  8.9 0.1 collective-permute-start.1
  9.0 0.6 dynamic-slice.1
  10.2 0.3 dynamic-update-slice
  10.5 5.0 %all-reduce = bf16[3200]{0:T(1024)(128)(2,1)S(1)} all-reduce(bf16[3200]{0:T(1024)(128)(2,1)S(1)} %dynamic-update-slice), channel_id=2, replica_groups=mesh['group'=16,'tp'=2] {'tp'}, use_global_device_ids=true, to_apply=%add | all-reduce | flops 3200 | bytes 12800
  15.6 1.0 broadcast_compare_fusion
  16.6 40.9 %all-gather.5.cloned.1.call-done = bf16[512,3200]{0,1:T(8,128)(2,1)} async-done(((bf16[512,1600]{0,1:T(8,128)(2,1)}), bf16[512,3200]{0,1:T(8,128)(2,1)}) %all-gather.5.cloned.1.call-update) | async-done | bytes 3276816 | tf_op jit(solution)/shard_map/all_gather | solution.py:25
  57.4 2.7 fusion.4
  60.1 101.9 %all-gather.7.cloned.1.call-done = bf16[3200,3,1024]{2,0,1:T(8,128)(2,1)} async-done(((bf16[200,3,1024]{2,0,1:T(8,128)(2,1)}), bf16[3200,3,1024]{2,0,1:T(8,128)(2,1)}) %all-gather.7.cloned.1.call-update) | async-done | bytes 19660816 | tf_op jit(solution)/shard_map/all_gather | solution.py:31
  162.1 24.0 %copy.25 = bf16[3200,3,1024]{0,2,1:T(8,128)(2,1)} copy(bf16[3200,3,1024]{2,0,1:T(8,128)(2,1)} %all-gather.7.cloned.1.call-done) | data formatting | bytes 39321600 | tf_op jit(solution)/shard_map/all_gather | solution.py:31
  186.0 17.9 %fusion.1 = f32[512,3,1024]{2,0,1:T(8,128)} fusion(bf16[3200,3,1024]{0,2,1:T(8,128)(2,1)} %copy.25, bf16[512,3200]{0,1:T(8,128)(2,1)S(1)} %copy-done.2, f32[3200]{0:T(1024)S(1)} %mul.120, f32[512]{0:T(512)S(1)} %add_rsqrt_fusion.2), kind=kOutput, calls=%fused_computation.2 | convolution fusion | flops 10072883200 | bytes 29243904 | tf_op jit(solution)/shard_map/dot_general | solution.py:32
  203.9 1.7 slice.52
  205.7 5.1 %slice_bitcast_fusion = (f32[64,8,8,128]{3,1,2,0:T(8,128)S(1)}, f32[64,8,8,128]{3,1,2,0:T(8,128)}, f32[512]{0:T(512)S(1)}, f32[512,1024]{1,0:T(8,128)}) fusion(f32[512,3,1024]{2,0,1:T(8,128)} %fusion.1), kind=kLoop, calls=%fused_computation.31 | loop fusion | flops 1048064 | bytes 10487808
  210.7 0.5 copy.38
  211.2 1.8 multiply_reduce_fusion.1
  213.0 4.0 all-reduce.1
  217.0 0.1 dynamic-slice.2
  217.0 1.3 copy.36
  218.4 1.3 fusion.32
  219.7 0.1 pad_maximum_fusion
  219.8 1.5 collective-permute-start
  221.3 0.5 copy.39
  221.8 0.5 fusion.16
  222.3 0.5 collective-permute-done
  222.8 0.7 fusion.42
  223.6 1.8 copy.27
  225.3 0.8 copy.31
  226.2 1.1 copy.32
  227.3 5.4 %fusion.23 = f32[8,512,640]{2,1,0:T(8,128)} fusion(bf16[128,8,128]{2,0,1:T(8,128)(2,1)S(1)} %copy.32, bf16[512,8,128]{2,0,1:T(8,128)(2,1)S(1)} %fusion.16, f32[512,8,128]{2,1,0:T(8,128)S(1)} %bitcast.68, f32[8,128]{1,0:T(8,128)S(1)} %bitcast.76, f32[512]{0:T(512)S(1)} %add_rsqrt_fusion), kind=kOutput, calls=%fused_computation.38 | convolution fusion | flops 675282944 | bytes 13899776 | tf_op jit(solution)/shard_map/qhd,khd->hqk/dot_general | solution.py:60
  232.8 15.3 %fusion.44 = (f32[8,512]{1,0:T(8,128)S(1)}, f32[8,512,640]{2,1,0:T(8,128)}) fusion(f32[8,512,640]{2,1,0:T(8,128)} %fusion.23, pred[512,640]{1,0:T(8,128)(4,1)S(1)} %copy-done.4), kind=kOutput, calls=%fused_computation.76 | output fusion | flops 15729279 | bytes 21315584 | tf_op jit(solution)/shard_map/sub | solution.py:66
  248.1 5.9 %fusion.19 = bf16[8,128,512]{2,1,0:T(8,128)(2,1)S(1)} fusion(f32[8,512,640]{2,1,0:T(8,128)} %get-tuple-element.16, f32[8,512]{1,0:T(8,128)S(1)} %get-tuple-element.15, bf16[128,8,128]{0,2,1:T(8,128)(2,1)S(1)} %bitcast.71, bf16[512,8,128]{0,2,1:T(8,128)(2,1)S(1)} %bitcast.69), kind=kOutput, calls=%fused_computation.34 | convolution fusion | flops 679477248 | bytes 12861440 | tf_op jit(solution)/shard_map/hqk,khd->qhd/dot_general | solution.py:68
  254.1 7.8 %convolution_convert_fusion = bf16[512,3200]{0,1:T(8,128)(2,1)} fusion(bf16[1024,3200]{0,1:T(8,128)(2,1)} %all-gather.9.cloned.1.call-done, bf16[512,1024]{0,1:T(8,128)(2,1)S(1)} %bitcast.78), kind=kOutput, calls=%fused_computation.13 | convolution fusion | flops 3357081600 | bytes 10878976 | tf_op jit(solution)/shard_map/dot_general | solution.py:70
  261.9 0.7 copy-done.6
  262.5 1.3 reduce-window.6
  263.9 0.2 slice_reduce_fusion
  264.1 0.1 fusion.35
  264.3 42.3 %reduce-scatter.2.cloned.1.call-done = bf16[512,1600]{0,1:T(8,128)(2,1)} async-done(((bf16[512,3200]{0,1:T(8,128)(2,1)}), bf16[512,1600]{0,1:T(8,128)(2,1)}) %reduce-scatter.2.cloned.1.call-update) | async-done | bytes 1638416 | tf_op jit(solution)/shard_map/reduce_scatter | solution.py:75
  306.6 2.0 add_convert_fusion
  308.6 2.3 copy.33
  310.9 0.4 broadcast_in_dim.16
  311.3 60.7 %scatter_fusion = bf16[16,64,1600]{2,1,0:T(8,128)(2,1)S(1)} fusion(bf16[16,64,1600]{2,1,0:T(8,128)(2,1)S(1)} %broadcast_in_dim.16, s32[512]{0:T(512)S(1)} %bitcast.65, bf16[512,1600]{1,0:T(8,128)(2,1)} %copy.33), kind=kCustom, calls=%fused_computation | custom fusion | bytes 4919296 | tf_op jit(solution)/shard_map/scatter | solution.py:86
  372.0 82.8 %all_to_all.5 = bf16[16,64,1600]{2,1,0:T(8,128)(2,1)S(1)} all-to-all(bf16[16,64,1600]{2,1,0:T(8,128)(2,1)S(1)} %scatter_fusion), channel_id=1, replica_groups=mesh['group'=16,'tp'=2] {'group'}, dimensions={0} | all-to-all | bytes 6553600 | tf_op jit(solution)/shard_map/all_to_all | solution.py:88
  454.8 1.8 copy.55
  (40 shorter events, 0.3 us)
Async XLA Ops:
  6.5 2.4 copy-start.11
  6.5 2.3 copy-start.8
  6.5 3.7 copy-start.10
  6.5 4.0 copy-start.9
  6.5 50.9 %all-gather.5.cloned.1.call-start = ((), (), s32[]{:S(2)}) async-start(), calls=%async_computation.2 | async-start | bytes 4915200 | tf_op jit(solution)/shard_map/all_gather | solution.py:25
  7.3 154.8 %all-gather.7.cloned.1.call-start = ((), (), s32[]{:S(2)}) async-start(), calls=%async_computation.3 | async-start | bytes 20889600 | tf_op jit(solution)/shard_map/all_gather | solution.py:31
  8.0 246.0 %all-gather.9.cloned.1.call-start = ((), (), s32[]{:S(2)}) async-start(), calls=%async_computation.4 | async-start | bytes 6963200 | tf_op jit(solution)/shard_map/all_gather | solution.py:72
  8.8 297.8 %reduce-scatter.2.cloned.1.call-start = ((), (), s32[]{:S(2)}) async-start(), calls=%async_computation.5 | async-start | bytes 4915200 | tf_op jit(solution)/shard_map/reduce_scatter | solution.py:75
  8.9 6.7 %collective-permute-start.1 = (s32[128]{0:T(128)S(1)}, s32[128]{0:T(128)S(1)}, u32[]{:S(2)}, u32[]{:S(2)}) collective-permute-start(s32[128]{0:T(128)S(1)} %dynamic_slice.11), channel_id=1, source_target_pairs={{0,2},{2,0},{4,6},{6,4},{8,10},{10,8},{12,14},{14,12},{16,18},{18,... | collective-permute-start | bytes 1544 | tf_op jit(solution)/shard_map/ppermute | solution.py:14
  60.1 125.9 %copy-start.2 = (bf16[512,3200]{0,1:T(8,128)(2,1)S(1)}, bf16[512,3200]{0,1:T(8,128)(2,1)}, u32[]{:S(2)}) copy-start(bf16[512,3200]{0,1:T(8,128)(2,1)} %all-gather.5.cloned.1.call-done) | copy-start | bytes 9830404
  218.4 2.9 copy-start
  219.8 3.0 collective-permute-start
  227.3 5.4 %copy-start.4 = (pred[512,640]{1,0:T(8,128)(4,1)S(1)}, pred[512,640]{1,0:T(8,128)(4,1)}, u32[]{:S(2)}) copy-start(pred[512,640]{1,0:T(8,128)(4,1)} %broadcast_compare_fusion) | copy-start | bytes 983044
  232.7 15.3 %copy-start.3 = (bf16[512,1,1024]{0,2,1:T(8,128)(2,1)S(1)}, bf16[512,1,1024]{0,2,1:T(8,128)(2,1)}, u32[]{:S(2)}) copy-start(bf16[512,1,1024]{0,2,1:T(8,128)(2,1)} %copy.36) | copy-start | bytes 3145732
  232.7 15.3 %copy-start.5 = (bf16[1,128,1024]{1,2,0:T(8,128)(2,1)S(1)}, bf16[1,128,1024]{1,2,0:T(8,128)(2,1)}, u32[]{:S(2)}) copy-start(bf16[1,128,1024]{1,2,0:T(8,128)(2,1)} %copy.27) | copy-start | bytes 786436
  261.8 0.7 copy-start.6
  261.8 44.7 %copy-start.1 = (bf16[512,1600]{0,1:T(8,128)(2,1)S(1)}, bf16[512,1600]{0,1:T(8,128)(2,1)}, u32[]{:S(2)}) copy-start(bf16[512,1600]{0,1:T(8,128)(2,1)} %param.8) | copy-start | bytes 4915204
  261.9 44.7 %copy-start.7 = (f32[1600]{0:T(1024)S(1)}, f32[1600]{0:T(1024)}, u32[]{:S(2)}) copy-start(f32[1600]{0:T(1024)} %param.13) | copy-start | bytes 19204
Sparse Core Ops, SparseCore 0:
  8.9 48.4 all-gather.4
  59.0 103.0 all-gather.6
  164.4 63.3 all-gather.8
  262.0 44.5 reduce-scatter.1
where the time goes:
time: 466 us; the launch traced here: 463 us
  waiting for transfers between devices  188 us (40%)
  local copies, waits for them, and re-layouts  99.5 us (21%)
  blocking collectives  91.8 us (20%)
  matrix products  37 us (8%)
  other arithmetic  31.2 us (7%)
  between operations  14 us (3%)
    all_gather x1, waiting for transfers between devices, shards(): piece = lax.all_gather(w_qkv, 'group', axis=0, tiled=True)  102 us
    all_to_all x1, blocking collectives, shards(): lax.all_to_all(outbox, 'group', split_axis=0, concat_axis=0, tiled=True)  82.8 us
    scatter x1, local copies, waits for them, and re-layouts, shards(): jnp.zeros((group_count, capacity, feat_local), jnp.bfloat16)  60.7 us
    reduce_scatter x1, waiting for transfers between devices, shards(): lax.psum_scatter(partial_terms.astype(jnp.bfloat16), 'tp', scatter_dimens...  42.3 us
    all_gather x1, waiting for transfers between devices, shards(): lax.all_gather(tokens, 'tp', axis=1, tiled=True)  40.9 us
    all_gather x1, local copies, waits for them, and re-layouts, shards(): piece = lax.all_gather(w_qkv, 'group', axis=0, tiled=True)  24 us
    dot_general x1, matrix products, shards(): jnp.dot(normed, piece.reshape(piece.shape[0], 3 * local_width), preferred...  17.9 us
    sub x1, other arithmetic, shards(): expo = jnp.exp(scores - top)  15.3 us
  transfers between devices with their start and end apart: 6, of which 4 were waited for; matrix products, arithmetic and copies ran while one was open for 20% of the time, Pallas kernels for 0%

commit v1 on v0

--- a/solution.py
+++ b/solution.py
@@ -28,7 +28,23 @@
     xwide = whole.astype(jnp.float32)
     stat = jnp.mean(xwide * xwide, axis=-1, keepdims=True)
     normed = (xwide * lax.rsqrt(stat + 1e-06) * gain_all.astype(jnp.float32)).astype(jnp.bfloat16)
-    piece = lax.all_gather(w_qkv, "group", axis=0, tiled=True)
+    peers, here, span = (lax.axis_size("group"), lax.axis_index("group"), w_qkv.shape[0])
+    upward = [(i, (i + 1) % peers) for i in range(peers)]
+    left = [(i, (i - 1) % peers) for i in range(peers)]
+    piece = jnp.zeros((*w_qkv.shape[:0], peers * span, *w_qkv.shape[0 + 1 :]), w_qkv.dtype)
+    piece = lax.dynamic_update_slice_in_dim(piece, w_qkv, here * span, axis=0)
+    from_left = from_right = w_qkv
+    halfway = peers // 2
+    for step in range(1, halfway + 1):
+        from_left = lax.ppermute(from_left, "group", upward)
+        piece = lax.dynamic_update_slice_in_dim(
+            piece, from_left, (here - step) % peers * span, axis=0
+        )
+        if step < peers - halfway:
+            from_right = lax.ppermute(from_right, "group", left)
+            piece = lax.dynamic_update_slice_in_dim(
+                piece, from_right, (here + step) % peers * span, axis=0
+            )
     qkv = jnp.dot(
         normed, piece.reshape(piece.shape[0], 3 * local_width), preferred_element_type=jnp.float32
     ).reshape(rows, 3, local_width)

time: 466 us -> 827 us (1.77)
  local copies, waits for them, and re-layouts: 99.5 us -> 372 us
  waiting for transfers between devices: 188 us -> 247 us
  starting transfers between devices: 1.72 us -> 23 us
    dynamic_update_slice x0 -> x16, local copies, waits for them, and re-layouts: none -> 264 us  [the longest x8 131 us: shards(): lax.dynamic_update_slice_in_dim(piece, from_left, (here - step) % peers *...]
    ppermute x0 -> x15, waiting for transfers between devices: none -> 206 us  [the longest x8 123 us: shards(): from_left = lax.ppermute(from_left, 'group', upward)]
    all_gather x1 -> x0, waiting for transfers between devices: 102 us -> none  [shards(): piece = lax.all_gather(w_qkv, 'group', axis=0, tiled=True)]
    all_gather x1, waiting for transfers between devices: 40.9 us -> 0.01 us  [shards(): lax.all_gather(tokens, 'tp', axis=1, tiled=True)]
    all_gather x1 -> x0, local copies, waits for them, and re-layouts: 24 us -> none  [shards(): piece = lax.all_gather(w_qkv, 'group', axis=0, tiled=True)]
    ppermute x0 -> x15, local copies, waits for them, and re-layouts: none -> 20.6 us  [the longest x8 12 us: shards(): from_left = lax.ppermute(from_left, 'group', upward)]
    ppermute x0 -> x15, starting transfers between devices: none -> 20.1 us  [the longest x8 20 us: shards(): from_left = lax.ppermute(from_left, 'group', upward)]
  transfers between devices with their start and end apart: 6 -> 20, of which waited for: 4 -> 14; matrix products, arithmetic and copies ran while one was open for 20% -> 44% of each run, Pallas kernels for 0% -> 0%
where the time goes in v1:
time: 827 us; the launch traced here: 816 us
  local copies, waits for them, and re-layouts  372 us (45%)
  waiting for transfers between devices  247 us (30%)
  blocking collectives  90.7 us (11%)
  matrix products  38 us (5%)
  other arithmetic  30.7 us (4%)
  starting transfers between devices  23 us (3%)
  between operations  14.7 us (2%)
    dynamic_update_slice x8, local copies, waits for them, and re-layouts, shards(): lax.dynamic_update_slice_in_dim(piece, from_left, (here - step) % peers *...  131 us
    ppermute x8, waiting for transfers between devices, shards(): from_left = lax.ppermute(from_left, 'group', upward)  123 us
    dynamic_update_slice x7, local copies, waits for them, and re-layouts, shards(): lax.dynamic_update_slice_in_dim(piece, from_right, (here + step) % peers...  117 us
    all_to_all x1, blocking collectives, shards(): lax.all_to_all(outbox, 'group', split_axis=0, concat_axis=0, tiled=True)  82.8 us
    ppermute x7, waiting for transfers between devices, shards(): from_right = lax.ppermute(from_right, 'group', left)  82.2 us
    scatter x1, local copies, waits for them, and re-layouts, shards(): jnp.zeros((group_count, capacity, feat_local), jnp.bfloat16)  60.7 us
    reduce_scatter x1, waiting for transfers between devices, shards(): lax.psum_scatter(partial_terms.astype(jnp.bfloat16), 'tp', scatter_dimens...  41.1 us
    ppermute x8, starting transfers between devices, shards(): from_left = lax.ppermute(from_left, 'group', upward)  20 us
  transfers between devices with their start and end apart: 20, of which 14 were waited for; matrix products, arithmetic and copies ran while one was open for 44% of the time, Pallas kernels for 0%

profile of v1, /device:TPU:1, one launch (start us, length us, event | category | flops | bytes accessed | tf_op | source)
XLA Modules:
  0.0 815.9 jit_solution(14622143040544029255)
XLA Ops:
  6.6 2.7 collective-permute-start
  9.3 27.2 %collective-permute-done = bf16[200,3,1024]{2,0,1:T(8,128)(2,1)} collective-permute-done((bf16[200,3,1024]{2,0,1:T(8,128)(2,1)}, bf16[200,3,1024]{2,0,1:T(8,128)(2,1)}, u32[]{:S(2)}, u32[]{:S(2)}) %collective-permute-start) | collective-permute-done | bytes 1228832 | tf_op jit(solution)/shard_map/ppermute | solution.py:39
  36.4 2.5 collective-permute-start.2
  39.0 13.4 %collective-permute-done.1 = bf16[200,3,1024]{2,0,1:T(8,128)(2,1)S(1)} collective-permute-done((bf16[200,3,1024]{2,0,1:T(8,128)(2,1)}, bf16[200,3,1024]{2,0,1:T(8,128)(2,1)S(1)}, u32[]{:S(2)}, u32[]{:S(2)}) %collective-permute-start.1) | collective-permute-done | bytes 1228832 | tf_op jit(solution)/shard_map/ppermute | solution.py:44
  52.4 12.9 %collective-permute-done.2 = bf16[200,3,1024]{2,0,1:T(8,128)(2,1)} collective-permute-done((bf16[200,3,1024]{2,0,1:T(8,128)(2,1)}, bf16[200,3,1024]{2,0,1:T(8,128)(2,1)}, u32[]{:S(2)}, u32[]{:S(2)}) %collective-permute-start.2) | collective-permute-done | bytes 1228832 | tf_op jit(solution)/shard_map/ppermute | solution.py:39
  65.2 2.5 collective-permute-start.4
  67.7 14.3 %collective-permute-done.3 = bf16[200,3,1024]{2,0,1:T(8,128)(2,1)S(1)} collective-permute-done((bf16[200,3,1024]{2,0,1:T(8,128)(2,1)S(1)}, bf16[200,3,1024]{2,0,1:T(8,128)(2,1)S(1)}, u32[]{:S(2)}, u32[]{:S(2)}) %collective-permute-start.3) | collective-permute-done | bytes 1228832 | tf_op jit(solution)/shard_map/ppermute | solution.py:44
  82.1 11.8 %collective-permute-done.4 = bf16[200,3,1024]{2,0,1:T(8,128)(2,1)S(1)} collective-permute-done((bf16[200,3,1024]{2,0,1:T(8,128)(2,1)}, bf16[200,3,1024]{2,0,1:T(8,128)(2,1)S(1)}, u32[]{:S(2)}, u32[]{:S(2)}) %collective-permute-start.4) | collective-permute-done | bytes 1228832 | tf_op jit(solution)/shard_map/ppermute | solution.py:39
  97.3 12.6 %collective-permute-done.5 = bf16[200,3,1024]{2,0,1:T(8,128)(2,1)} collective-permute-done((bf16[200,3,1024]{2,0,1:T(8,128)(2,1)S(1)}, bf16[200,3,1024]{2,0,1:T(8,128)(2,1)}, u32[]{:S(2)}, u32[]{:S(2)}) %collective-permute-start.5) | collective-permute-done | bytes 1228832 | tf_op jit(solution)/shard_map/ppermute | solution.py:44
  109.9 13.8 %collective-permute-done.6 = bf16[200,3,1024]{2,0,1:T(8,128)(2,1)} collective-permute-done((bf16[200,3,1024]{2,0,1:T(8,128)(2,1)S(1)}, bf16[200,3,1024]{2,0,1:T(8,128)(2,1)}, u32[]{:S(2)}, u32[]{:S(2)}) %collective-permute-start.6) | collective-permute-done | bytes 1228832 | tf_op jit(solution)/shard_map/ppermute | solution.py:39
  123.7 2.6 collective-permute-start.8
  126.3 14.9 %collective-permute-done.7 = bf16[200,3,1024]{2,0,1:T(8,128)(2,1)} collective-permute-done((bf16[200,3,1024]{2,0,1:T(8,128)(2,1)}, bf16[200,3,1024]{2,0,1:T(8,128)(2,1)}, u32[]{:S(2)}, u32[]{:S(2)}) %collective-permute-start.7) | collective-permute-done | bytes 1228832 | tf_op jit(solution)/shard_map/ppermute | solution.py:44
  141.2 14.5 %collective-permute-done.8 = bf16[200,3,1024]{2,0,1:T(8,128)(2,1)} collective-permute-done((bf16[200,3,1024]{2,0,1:T(8,128)(2,1)}, bf16[200,3,1024]{2,0,1:T(8,128)(2,1)}, u32[]{:S(2)}, u32[]{:S(2)}) %collective-permute-start.8) | collective-permute-done | bytes 1228832 | tf_op jit(solution)/shard_map/ppermute | solution.py:39
  158.2 19.1 %collective-permute-done.9 = bf16[200,3,1024]{2,0,1:T(8,128)(2,1)S(1)} collective-permute-done((bf16[200,3,1024]{2,0,1:T(8,128)(2,1)}, bf16[200,3,1024]{2,0,1:T(8,128)(2,1)S(1)}, u32[]{:S(2)}, u32[]{:S(2)}) %collective-permute-start.9) | collective-permute-done | bytes 1228832 | tf_op jit(solution)/shard_map/ppermute | solution.py:44
  178.4 24.5 %collective-permute-done.10 = bf16[200,3,1024]{2,0,1:T(8,128)(2,1)S(1)} collective-permute-done((bf16[200,3,1024]{2,0,1:T(8,128)(2,1)}, bf16[200,3,1024]{2,0,1:T(8,128)(2,1)S(1)}, u32[]{:S(2)}, u32[]{:S(2)}) %collective-permute-start.10) | collective-permute-done | bytes 1228832 | tf_op jit(solution)/shard_map/ppermute | solution.py:39
  205.3 7.9 collective-permute-done.11
  213.2 18.8 %collective-permute-done.12 = bf16[200,3,1024]{2,0,1:T(8,128)(2,1)} collective-permute-done((bf16[200,3,1024]{2,0,1:T(8,128)(2,1)S(1)}, bf16[200,3,1024]{2,0,1:T(8,128)(2,1)}, u32[]{:S(2)}, u32[]{:S(2)}) %collective-permute-start.12) | collective-permute-done | bytes 1228832 | tf_op jit(solution)/shard_map/ppermute | solution.py:39
  232.0 2.6 collective-permute-start.14
  237.8 4.1 all-reduce
  242.0 6.9 broadcast_in_dim.19
  248.9 16.6 %dynamic_update_slice.48 = bf16[3200,3,1024]{0,2,1:T(8,128)(2,1)} dynamic-update-slice(bf16[3200,3,1024]{0,2,1:T(8,128)(2,1)} %broadcast_in_dim.19, bf16[200,3,1024]{0,2,1:T(8,128)(2,1)S(1)} %copy.27, s32[]{:T(128)S(6)} %select_n.142, s32[]{:T(128)} %constant.121.clone.1, s32[]{:T(128)} %constant.121.clone.1) | dynamic-update-slice | bytes 2457604 | tf_op jit(solution)/shard_map/dynamic_update_slice | solution.py:35
  268.3 14.8 %dynamic_update_slice.49 = bf16[3200,3,1024]{0,2,1:T(8,128)(2,1)} dynamic-update-slice(bf16[3200,3,1024]{0,2,1:T(8,128)(2,1)} %dynamic_update_slice.48, bf16[200,3,1024]{0,2,1:T(8,128)(2,1)S(1)} %copy.28, s32[]{:T(128)S(6)} %select_n.144, s32[]{:T(128)} %constant.121.clone.1, s32[]{:T(128)} %constant.121.clone.1) | dynamic-update-slice | bytes 2457604 | tf_op jit(solution)/shard_map/dynamic_update_slice | solution.py:40
  283.8 16.6 %dynamic_update_slice.50 = bf16[3200,3,1024]{0,2,1:T(8,128)(2,1)} dynamic-update-slice(bf16[3200,3,1024]{0,2,1:T(8,128)(2,1)} %dynamic_update_slice.49, bf16[200,3,1024]{0,2,1:T(8,128)(2,1)S(1)} %copy.29, s32[]{:T(128)S(6)} %select_n.146, s32[]{:T(128)} %constant.121.clone.1, s32[]{:T(128)} %constant.121.clone.1) | dynamic-update-slice | bytes 2457604 | tf_op jit(solution)/shard_map/dynamic_update_slice | solution.py:45
  302.2 15.9 %dynamic_update_slice.51 = bf16[3200,3,1024]{0,2,1:T(8,128)(2,1)} dynamic-update-slice(bf16[3200,3,1024]{0,2,1:T(8,128)(2,1)} %dynamic_update_slice.50, bf16[200,3,1024]{0,2,1:T(8,128)(2,1)S(1)} %copy.30, s32[]{:T(128)S(6)} %select_n.148, s32[]{:T(128)} %constant.121.clone.1, s32[]{:T(128)} %constant.121.clone.1) | dynamic-update-slice | bytes 2457604 | tf_op jit(solution)/shard_map/dynamic_update_slice | solution.py:40
  318.7 16.8 %dynamic_update_slice.52 = bf16[3200,3,1024]{0,2,1:T(8,128)(2,1)} dynamic-update-slice(bf16[3200,3,1024]{0,2,1:T(8,128)(2,1)} %dynamic_update_slice.51, bf16[200,3,1024]{0,2,1:T(8,128)(2,1)S(1)} %copy.31, s32[]{:T(128)S(6)} %select_n.150, s32[]{:T(128)} %constant.121.clone.1, s32[]{:T(128)} %constant.121.clone.1) | dynamic-update-slice | bytes 2457604 | tf_op jit(solution)/shard_map/dynamic_update_slice | solution.py:45
  335.5 2.7 fusion.4
  338.8 16.7 %dynamic_update_slice.53 = bf16[3200,3,1024]{0,2,1:T(8,128)(2,1)} dynamic-update-slice(bf16[3200,3,1024]{0,2,1:T(8,128)(2,1)} %dynamic_update_slice.52, bf16[200,3,1024]{0,2,1:T(8,128)(2,1)S(1)} %copy.32, s32[]{:T(128)S(6)} %select_n.152, s32[]{:T(128)} %constant.121.clone.1, s32[]{:T(128)} %constant.121.clone.1) | dynamic-update-slice | bytes 2457604 | tf_op jit(solution)/shard_map/dynamic_update_slice | solution.py:40
  357.2 16.6 %dynamic_update_slice.54 = bf16[3200,3,1024]{0,2,1:T(8,128)(2,1)} dynamic-update-slice(bf16[3200,3,1024]{0,2,1:T(8,128)(2,1)} %dynamic_update_slice.53, bf16[200,3,1024]{0,2,1:T(8,128)(2,1)S(1)} %copy.33, s32[]{:T(128)S(6)} %select_n.154, s32[]{:T(128)} %constant.121.clone.1, s32[]{:T(128)} %constant.121.clone.1) | dynamic-update-slice | bytes 2457604 | tf_op jit(solution)/shard_map/dynamic_update_slice | solution.py:45
  375.4 16.7 %dynamic_update_slice.55 = bf16[3200,3,1024]{0,2,1:T(8,128)(2,1)} dynamic-update-slice(bf16[3200,3,1024]{0,2,1:T(8,128)(2,1)} %dynamic_update_slice.54, bf16[200,3,1024]{0,2,1:T(8,128)(2,1)S(1)} %copy.34, s32[]{:T(128)S(6)} %select_n.156, s32[]{:T(128)} %constant.121.clone.1, s32[]{:T(128)} %constant.121.clone.1) | dynamic-update-slice | bytes 2457604 | tf_op jit(solution)/shard_map/dynamic_update_slice | solution.py:40
  393.7 16.7 %dynamic_update_slice.56 = bf16[3200,3,1024]{0,2,1:T(8,128)(2,1)} dynamic-update-slice(bf16[3200,3,1024]{0,2,1:T(8,128)(2,1)} %dynamic_update_slice.55, bf16[200,3,1024]{0,2,1:T(8,128)(2,1)S(1)} %copy.35, s32[]{:T(128)S(6)} %select_n.158, s32[]{:T(128)} %constant.121.clone.1, s32[]{:T(128)} %constant.121.clone.1) | dynamic-update-slice | bytes 2457604 | tf_op jit(solution)/shard_map/dynamic_update_slice | solution.py:45
  412.2 16.6 %dynamic_update_slice.57 = bf16[3200,3,1024]{0,2,1:T(8,128)(2,1)} dynamic-update-slice(bf16[3200,3,1024]{0,2,1:T(8,128)(2,1)} %dynamic_update_slice.56, bf16[200,3,1024]{0,2,1:T(8,128)(2,1)S(1)} %copy.36, s32[]{:T(128)S(6)} %select_n.160, s32[]{:T(128)} %constant.121.clone.1, s32[]{:T(128)} %constant.121.clone.1) | dynamic-update-slice | bytes 2457604 | tf_op jit(solution)/shard_map/dynamic_update_slice | solution.py:40
  429.5 16.7 %dynamic_update_slice.58 = bf16[3200,3,1024]{0,2,1:T(8,128)(2,1)} dynamic-update-slice(bf16[3200,3,1024]{0,2,1:T(8,128)(2,1)} %dynamic_update_slice.57, bf16[200,3,1024]{0,2,1:T(8,128)(2,1)S(1)} %copy.37, s32[]{:T(128)S(6)} %select_n.162, s32[]{:T(128)} %constant.121.clone.1, s32[]{:T(128)} %constant.121.clone.1) | dynamic-update-slice | bytes 2457604 | tf_op jit(solution)/shard_map/dynamic_update_slice | solution.py:45
  446.9 16.6 %dynamic_update_slice.59 = bf16[3200,3,1024]{0,2,1:T(8,128)(2,1)} dynamic-update-slice(bf16[3200,3,1024]{0,2,1:T(8,128)(2,1)} %dynamic_update_slice.58, bf16[200,3,1024]{0,2,1:T(8,128)(2,1)S(1)} %copy.38, s32[]{:T(128)S(6)} %select_n.164, s32[]{:T(128)} %constant.121.clone.1, s32[]{:T(128)} %constant.121.clone.1) | dynamic-update-slice | bytes 2457604 | tf_op jit(solution)/shard_map/dynamic_update_slice | solution.py:40
  465.2 16.7 %dynamic_update_slice.60 = bf16[3200,3,1024]{0,2,1:T(8,128)(2,1)} dynamic-update-slice(bf16[3200,3,1024]{0,2,1:T(8,128)(2,1)} %dynamic_update_slice.59, bf16[200,3,1024]{0,2,1:T(8,128)(2,1)S(1)} %copy.39, s32[]{:T(128)S(6)} %select_n.166, s32[]{:T(128)} %constant.121.clone.1, s32[]{:T(128)} %constant.121.clone.1) | dynamic-update-slice | bytes 2457604 | tf_op jit(solution)/shard_map/dynamic_update_slice | solution.py:45
  483.5 16.6 %dynamic_update_slice.61 = bf16[3200,3,1024]{0,2,1:T(8,128)(2,1)} dynamic-update-slice(bf16[3200,3,1024]{0,2,1:T(8,128)(2,1)} %dynamic_update_slice.60, bf16[200,3,1024]{0,2,1:T(8,128)(2,1)S(1)} %copy.40, s32[]{:T(128)S(6)} %select_n.168, s32[]{:T(128)} %constant.121.clone.1, s32[]{:T(128)} %constant.121.clone.1) | dynamic-update-slice | bytes 2457604 | tf_op jit(solution)/shard_map/dynamic_update_slice | solution.py:40
  501.8 16.7 %dynamic_update_slice.62 = bf16[3200,3,1024]{0,2,1:T(8,128)(2,1)} dynamic-update-slice(bf16[3200,3,1024]{0,2,1:T(8,128)(2,1)} %dynamic_update_slice.61, bf16[200,3,1024]{0,2,1:T(8,128)(2,1)S(1)} %copy.41, s32[]{:T(128)S(6)} %select_n.170, s32[]{:T(128)} %constant.121.clone.1, s32[]{:T(128)} %constant.121.clone.1) | dynamic-update-slice | bytes 2457604 | tf_op jit(solution)/shard_map/dynamic_update_slice | solution.py:45
  520.6 16.6 %dynamic_update_slice.63 = bf16[3200,3,1024]{0,2,1:T(8,128)(2,1)} dynamic-update-slice(bf16[3200,3,1024]{0,2,1:T(8,128)(2,1)} %dynamic_update_slice.62, bf16[200,3,1024]{0,2,1:T(8,128)(2,1)S(1)} %copy.42, s32[]{:T(128)S(6)} %select_n.172, s32[]{:T(128)} %constant.121.clone.1, s32[]{:T(128)} %constant.121.clone.1) | dynamic-update-slice | bytes 2457604 | tf_op jit(solution)/shard_map/dynamic_update_slice | solution.py:40
  537.2 18.8 %fusion.1 = f32[512,3,1024]{2,0,1:T(8,128)} fusion(bf16[3200,3,1024]{0,2,1:T(8,128)(2,1)} %dynamic_update_slice.63, bf16[512,3200]{0,1:T(8,128)(2,1)} %all-gather.4.cloned.1.call-done, f32[3200]{0:T(1024)S(1)} %mul.184, f32[512]{0:T(512)S(1)} %add_rsqrt_fusion.2), kind=kOutput, calls=%fused_computation.2 | convolution fusion | flops 10072883200 | bytes 29243904 | tf_op jit(solution)/shard_map/dot_general | solution.py:48
  557.8 4.5 slice_bitcast_fusion
  564.6 3.8 all-reduce.1
  571.3 2.9 collective-permute-start.15
  581.0 5.5 fusion.23
  586.5 15.4 %fusion.44 = (f32[8,512]{1,0:T(8,128)S(1)}, f32[8,512,640]{2,1,0:T(8,128)}) fusion(f32[8,512,640]{2,1,0:T(8,128)} %fusion.23, pred[512,640]{1,0:T(8,128)(4,1)S(1)} %copy-done.15), kind=kOutput, calls=%fused_computation.76 | output fusion | flops 15729279 | bytes 21315584 | tf_op jit(solution)/shard_map/sub | solution.py:82
  601.9 5.9 fusion.19
  607.9 7.8 convolution_convert_fusion
  618.1 41.1 %reduce-scatter.2.cloned.1.call-done = bf16[512,1600]{0,1:T(8,128)(2,1)} async-done(((bf16[512,3200]{0,1:T(8,128)(2,1)}), bf16[512,1600]{0,1:T(8,128)(2,1)}) %reduce-scatter.2.cloned.1.call-update) | async-done | bytes 1638416 | tf_op jit(solution)/shard_map/reduce_scatter | solution.py:91
  663.9 60.7 %scatter_fusion = bf16[16,64,1600]{2,1,0:T(8,128)(2,1)S(1)} fusion(bf16[16,64,1600]{2,1,0:T(8,128)(2,1)S(1)} %broadcast_in_dim.18, s32[512]{0:T(512)S(1)} %bitcast.64, bf16[512,1600]{1,0:T(8,128)(2,1)} %copy.50), kind=kCustom, calls=%fused_computation | custom fusion | bytes 4919296 | tf_op jit(solution)/shard_map/scatter | solution.py:102
  724.6 82.8 %all_to_all.5 = bf16[16,64,1600]{2,1,0:T(8,128)(2,1)S(1)} all-to-all(bf16[16,64,1600]{2,1,0:T(8,128)(2,1)S(1)} %scatter_fusion), channel_id=1, replica_groups=mesh['group'=16,'tp'=2] {'group'}, dimensions={0} | all-to-all | bytes 6553600 | tf_op jit(solution)/shard_map/all_to_all | solution.py:104
  (121 shorter events, 56.0 us)
Async XLA Ops:
  6.5 228.8 %copy-start.3 = (bf16[200,3,1024]{2,0,1:T(8,128)(2,1)S(1)}, bf16[200,3,1024]{2,0,1:T(8,128)(2,1)}, u32[]{:S(2)}) copy-start(bf16[200,3,1024]{2,0,1:T(8,128)(2,1)} %param.10) | copy-start | bytes 3686404
  6.5 229.7 %copy-start.22 = (u32[32]{0:T(128)S(1)}, u32[32]{0:T(128)}, u32[]{:S(2)}) copy-start(u32[32]{0:T(128)} %constant.171) | copy-start | bytes 388
  6.5 231.0 %copy-start.21 = (bf16[1600]{0:T(1024)(128)(2,1)S(1)}, bf16[1600]{0:T(1024)(128)(2,1)}, u32[]{:S(2)}) copy-start(bf16[1600]{0:T(1024)(128)(2,1)} %param.9) | copy-start | bytes 9604
  6.5 235.4 %copy-start.20 = (f32[2,1024]{1,0:T(2,128)S(1)}, f32[2,1024]{1,0:T(2,128)}, u32[]{:S(2)}) copy-start(f32[2,1024]{1,0:T(2,128)} %param.11) | copy-start | bytes 24580
  6.5 328.9 %all-gather.4.cloned.1.call-start = ((), (), s32[]{:S(2)}) async-start(), calls=%async_computation.2 | async-start | bytes 4915200 | tf_op jit(solution)/shard_map/all_gather | solution.py:25
  6.6 29.8 %collective-permute-start = (bf16[200,3,1024]{2,0,1:T(8,128)(2,1)}, bf16[200,3,1024]{2,0,1:T(8,128)(2,1)}, u32[]{:S(2)}, u32[]{:S(2)}) collective-permute-start(bf16[200,3,1024]{2,0,1:T(8,128)(2,1)} %param.10), channel_id=1, source_target_pairs={{0,2},{2,4},{4,6},{6,8},{8,10},{10,12},{12,14},{14,16},{16,18},{18... | collective-permute-start | bytes 3686408 | tf_op jit(solution)/shard_map/ppermute | solution.py:39
  9.3 43.1 %collective-permute-start.1 = (bf16[200,3,1024]{2,0,1:T(8,128)(2,1)}, bf16[200,3,1024]{2,0,1:T(8,128)(2,1)S(1)}, u32[]{:S(2)}, u32[]{:S(2)}) collective-permute-start(bf16[200,3,1024]{2,0,1:T(8,128)(2,1)} %param.10), channel_id=1, source_target_pairs={{0,30},{2,0},{4,2},{6,4},{8,6},{10,8},{12,10},{14,12},{16,14},{18,... | collective-permute-start | bytes 3686408 | tf_op jit(solution)/shard_map/ppermute | solution.py:44
  36.4 28.8 %collective-permute-start.2 = (bf16[200,3,1024]{2,0,1:T(8,128)(2,1)}, bf16[200,3,1024]{2,0,1:T(8,128)(2,1)}, u32[]{:S(2)}, u32[]{:S(2)}) collective-permute-start(bf16[200,3,1024]{2,0,1:T(8,128)(2,1)} %collective-permute-done), channel_id=1, source_target_pairs={{0,2},{2,4},{4,6},{6,8},{8,10},{10,12},{12,14},{14,16},{16,18},{18... | collective-permute-start | bytes 3686408 | tf_op jit(solution)/shard_map/ppermute | solution.py:39
  38.9 569.0 %all-gather.6.cloned.1.call-start = ((), (), s32[]{:S(2)}) async-start(), calls=%async_computation.3 | async-start | bytes 6963200 | tf_op jit(solution)/shard_map/all_gather | solution.py:88
  52.4 183.0 %copy-start.4 = (bf16[200,3,1024]{2,0,1:T(8,128)(2,1)}, bf16[200,3,1024]{2,0,1:T(8,128)(2,1)S(1)}, u32[]{:S(2)}) copy-start(bf16[200,3,1024]{2,0,1:T(8,128)(2,1)S(1)} %collective-permute-done.1) | copy-start | bytes 3686404
  52.4 29.7 %collective-permute-start.3 = (bf16[200,3,1024]{2,0,1:T(8,128)(2,1)S(1)}, bf16[200,3,1024]{2,0,1:T(8,128)(2,1)S(1)}, u32[]{:S(2)}, u32[]{:S(2)}) collective-permute-start(bf16[200,3,1024]{2,0,1:T(8,128)(2,1)S(1)} %collective-permute-done.1), channel_id=1, source_target_pairs={{0,30},{2,0},{4,2},{6,4},{8,6},{10,8},{12,10},{14,12},{16,14},{18,... | collective-permute-start | bytes 3686408 | tf_op jit(solution)/shard_map/ppermute | solution.py:44
  65.2 28.7 %collective-permute-start.4 = (bf16[200,3,1024]{2,0,1:T(8,128)(2,1)}, bf16[200,3,1024]{2,0,1:T(8,128)(2,1)S(1)}, u32[]{:S(2)}, u32[]{:S(2)}) collective-permute-start(bf16[200,3,1024]{2,0,1:T(8,128)(2,1)} %collective-permute-done.2), channel_id=1, source_target_pairs={{0,2},{2,4},{4,6},{6,8},{8,10},{10,12},{12,14},{14,16},{16,18},{18... | collective-permute-start | bytes 3686408 | tf_op jit(solution)/shard_map/ppermute | solution.py:39
  82.0 41.6 %copy-start.8 = (bf16[200,3,1024]{2,0,1:T(8,128)(2,1)}, bf16[200,3,1024]{2,0,1:T(8,128)(2,1)S(1)}, u32[]{:S(2)}) copy-start(bf16[200,3,1024]{2,0,1:T(8,128)(2,1)S(1)} %collective-permute-done.3) | copy-start | bytes 3686404
  82.0 27.9 %collective-permute-start.5 = (bf16[200,3,1024]{2,0,1:T(8,128)(2,1)S(1)}, bf16[200,3,1024]{2,0,1:T(8,128)(2,1)}, u32[]{:S(2)}, u32[]{:S(2)}) collective-permute-start(bf16[200,3,1024]{2,0,1:T(8,128)(2,1)S(1)} %collective-permute-done.3), channel_id=1, source_target_pairs={{0,30},{2,0},{4,2},{6,4},{8,6},{10,8},{12,10},{14,12},{16,14},{18,... | collective-permute-start | bytes 3686408 | tf_op jit(solution)/shard_map/ppermute | solution.py:44
  93.9 1.0 copy-start.6
  94.9 28.8 %collective-permute-start.6 = (bf16[200,3,1024]{2,0,1:T(8,128)(2,1)S(1)}, bf16[200,3,1024]{2,0,1:T(8,128)(2,1)}, u32[]{:S(2)}, u32[]{:S(2)}) collective-permute-start(bf16[200,3,1024]{2,0,1:T(8,128)(2,1)S(1)} %collective-permute-done.4), channel_id=1, source_target_pairs={{0,2},{2,4},{4,6},{6,8},{8,10},{10,12},{12,14},{14,16},{16,18},{18... | collective-permute-start | bytes 3686408 | tf_op jit(solution)/shard_map/ppermute | solution.py:39
  109.9 31.3 %collective-permute-start.7 = (bf16[200,3,1024]{2,0,1:T(8,128)(2,1)}, bf16[200,3,1024]{2,0,1:T(8,128)(2,1)}, u32[]{:S(2)}, u32[]{:S(2)}) collective-permute-start(bf16[200,3,1024]{2,0,1:T(8,128)(2,1)} %collective-permute-done.5), channel_id=1, source_target_pairs={{0,30},{2,0},{4,2},{6,4},{8,6},{10,8},{12,10},{14,12},{16,14},{18,... | collective-permute-start | bytes 3686408 | tf_op jit(solution)/shard_map/ppermute | solution.py:44
  123.7 32.0 %collective-permute-start.8 = (bf16[200,3,1024]{2,0,1:T(8,128)(2,1)}, bf16[200,3,1024]{2,0,1:T(8,128)(2,1)}, u32[]{:S(2)}, u32[]{:S(2)}) collective-permute-start(bf16[200,3,1024]{2,0,1:T(8,128)(2,1)} %collective-permute-done.6), channel_id=1, source_target_pairs={{0,2},{2,4},{4,6},{6,8},{8,10},{10,12},{12,14},{14,16},{16,18},{18... | collective-permute-start | bytes 3686408 | tf_op jit(solution)/shard_map/ppermute | solution.py:39
  126.3 532.9 %reduce-scatter.2.cloned.1.call-start = ((), (), s32[]{:S(2)}) async-start(), calls=%async_computation.4 | async-start | bytes 4915200 | tf_op jit(solution)/shard_map/reduce_scatter | solution.py:91
  141.2 36.1 %collective-permute-start.9 = (bf16[200,3,1024]{2,0,1:T(8,128)(2,1)}, bf16[200,3,1024]{2,0,1:T(8,128)(2,1)S(1)}, u32[]{:S(2)}, u32[]{:S(2)}) collective-permute-start(bf16[200,3,1024]{2,0,1:T(8,128)(2,1)} %collective-permute-done.7), channel_id=1, source_target_pairs={{0,30},{2,0},{4,2},{6,4},{8,6},{10,8},{12,10},{14,12},{16,14},{18,... | collective-permute-start | bytes 3686408 | tf_op jit(solution)/shard_map/ppermute | solution.py:44
  155.7 47.2 %collective-permute-start.10 = (bf16[200,3,1024]{2,0,1:T(8,128)(2,1)}, bf16[200,3,1024]{2,0,1:T(8,128)(2,1)S(1)}, u32[]{:S(2)}, u32[]{:S(2)}) collective-permute-start(bf16[200,3,1024]{2,0,1:T(8,128)(2,1)} %collective-permute-done.8), channel_id=1, source_target_pairs={{0,2},{2,4},{4,6},{6,8},{8,10},{10,12},{12,14},{14,16},{16,18},{18... | collective-permute-start | bytes 3686408 | tf_op jit(solution)/shard_map/ppermute | solution.py:39
  177.3 1.0 copy-start.10
  178.4 34.8 %collective-permute-start.11 = (bf16[200,3,1024]{2,0,1:T(8,128)(2,1)S(1)}, bf16[200,3,1024]{2,0,1:T(8,128)(2,1)}, u32[]{:S(2)}, u32[]{:S(2)}) collective-permute-start(bf16[200,3,1024]{2,0,1:T(8,128)(2,1)S(1)} %collective-permute-done.9), channel_id=1, source_target_pairs={{0,30},{2,0},{4,2},{6,4},{8,6},{10,8},{12,10},{14,12},{16,14},{18,... | collective-permute-start | bytes 3686408 | tf_op jit(solution)/shard_map/ppermute | solution.py:44
  202.9 10.2 %copy-start.12 = (bf16[200,3,1024]{2,0,1:T(8,128)(2,1)}, bf16[200,3,1024]{2,0,1:T(8,128)(2,1)S(1)}, u32[]{:S(2)}) copy-start(bf16[200,3,1024]{2,0,1:T(8,128)(2,1)S(1)} %collective-permute-done.10) | copy-start | bytes 3686404
  202.9 29.1 %collective-permute-start.12 = (bf16[200,3,1024]{2,0,1:T(8,128)(2,1)S(1)}, bf16[200,3,1024]{2,0,1:T(8,128)(2,1)}, u32[]{:S(2)}, u32[]{:S(2)}) collective-permute-start(bf16[200,3,1024]{2,0,1:T(8,128)(2,1)S(1)} %collective-permute-done.10), channel_id=1, source_target_pairs={{0,2},{2,4},{4,6},{6,8},{8,10},{10,12},{12,14},{14,16},{16,18},{18... | collective-permute-start | bytes 3686408 | tf_op jit(solution)/shard_map/ppermute | solution.py:39
  213.2 287.0 %collective-permute-start.13 = (bf16[200,3,1024]{2,0,1:T(8,128)(2,1)}, bf16[200,3,1024]{2,0,1:T(8,128)(2,1)}, u32[]{:S(2)}, u32[]{:S(2)}) collective-permute-start(bf16[200,3,1024]{2,0,1:T(8,128)(2,1)} %collective-permute-done.11), channel_id=1, source_target_pairs={{0,30},{2,0},{4,2},{6,4},{8,6},{10,8},{12,10},{14,12},{16,14},{18,... | collective-permute-start | bytes 3686408 | tf_op jit(solution)/shard_map/ppermute | solution.py:44
  232.0 286.5 %collective-permute-start.14 = (bf16[200,3,1024]{2,0,1:T(8,128)(2,1)}, bf16[200,3,1024]{2,0,1:T(8,128)(2,1)}, u32[]{:S(2)}, u32[]{:S(2)}) collective-permute-start(bf16[200,3,1024]{2,0,1:T(8,128)(2,1)} %collective-permute-done.12), channel_id=1, source_target_pairs={{0,2},{2,4},{4,6},{6,8},{8,10},{10,12},{12,14},{14,16},{16,18},{18... | collective-permute-start | bytes 3686408 | tf_op jit(solution)/shard_map/ppermute | solution.py:39
  235.3 30.2 %collective-permute-start.16 = (s32[128]{0:T(128)S(1)}, s32[128]{0:T(128)S(1)}, u32[]{:S(2)}, u32[]{:S(2)}) collective-permute-start(s32[128]{0:T(128)S(1)} %dynamic_slice.11), channel_id=1, source_target_pairs={{0,2},{2,0},{4,6},{6,4},{8,10},{10,8},{12,14},{14,12},{16,18},{18,... | collective-permute-start | bytes 1544 | tf_op jit(solution)/shard_map/ppermute | solution.py:14
  248.9 16.6 %copy-start.19 = (s32[512]{0:T(512)S(1)}, s32[512]{0:T(512)}, u32[]{:S(2)}) copy-start(s32[512]{0:T(512)} %param.14) | copy-start | bytes 6148
  266.5 16.6 %copy-start.5 = (bf16[200,3,1024]{2,0,1:T(8,128)(2,1)S(1)}, bf16[200,3,1024]{2,0,1:T(8,128)(2,1)}, u32[]{:S(2)}) copy-start(bf16[200,3,1024]{2,0,1:T(8,128)(2,1)} %copy-done.4) | copy-start | bytes 3686404
  300.4 17.6 %copy-start.9 = (bf16[200,3,1024]{2,0,1:T(8,128)(2,1)S(1)}, bf16[200,3,1024]{2,0,1:T(8,128)(2,1)}, u32[]{:S(2)}) copy-start(bf16[200,3,1024]{2,0,1:T(8,128)(2,1)} %copy-done.8) | copy-start | bytes 3686404
  318.7 19.5 %copy-start.7 = (bf16[200,3,1024]{2,0,1:T(8,128)(2,1)S(1)}, bf16[200,3,1024]{2,0,1:T(8,128)(2,1)}, u32[]{:S(2)}) copy-start(bf16[200,3,1024]{2,0,1:T(8,128)(2,1)} %copy-done.6) | copy-start | bytes 3686404
  410.4 18.4 %copy-start.11 = (bf16[200,3,1024]{2,0,1:T(8,128)(2,1)S(1)}, bf16[200,3,1024]{2,0,1:T(8,128)(2,1)}, u32[]{:S(2)}) copy-start(bf16[200,3,1024]{2,0,1:T(8,128)(2,1)} %copy-done.10) | copy-start | bytes 3686404
  429.5 16.7 %copy-start.13 = (bf16[200,3,1024]{2,0,1:T(8,128)(2,1)S(1)}, bf16[200,3,1024]{2,0,1:T(8,128)(2,1)}, u32[]{:S(2)}) copy-start(bf16[200,3,1024]{2,0,1:T(8,128)(2,1)} %copy-done.12) | copy-start | bytes 3686404
  569.9 4.3 copy-start
  571.3 5.2 collective-permute-start.15
  576.5 4.5 copy-start.1
  581.0 5.5 copy-start.15
  586.5 15.4 %copy-start.14 = (bf16[512,1,1024]{0,2,1:T(8,128)(2,1)S(1)}, bf16[512,1,1024]{0,2,1:T(8,128)(2,1)}, u32[]{:S(2)}) copy-start(bf16[512,1,1024]{0,2,1:T(8,128)(2,1)} %copy.53) | copy-start | bytes 3145732
  586.5 15.4 %copy-start.16 = (bf16[1,128,1024]{1,2,0:T(8,128)(2,1)S(1)}, bf16[1,128,1024]{1,2,0:T(8,128)(2,1)}, u32[]{:S(2)}) copy-start(bf16[1,128,1024]{1,2,0:T(8,128)(2,1)} %copy.44) | copy-start | bytes 786436
  615.7 0.7 copy-start.17
  615.7 43.5 %copy-start.2 = (bf16[512,1600]{0,1:T(8,128)(2,1)S(1)}, bf16[512,1600]{0,1:T(8,128)(2,1)}, u32[]{:S(2)}) copy-start(bf16[512,1600]{0,1:T(8,128)(2,1)} %param.8) | copy-start | bytes 4915204
  615.7 43.5 %copy-start.18 = (f32[1600]{0:T(1024)S(1)}, f32[1600]{0:T(1024)}, u32[]{:S(2)}) copy-start(f32[1600]{0:T(1024)} %param.13) | copy-start | bytes 19204
Sparse Core Ops, SparseCore 0:
  39.0 46.1 all-gather.3
  126.4 92.2 all-gather.5
  615.8 43.3 reduce-scatter.1
